TPU v7x, 32 devices: a whole 2x2x4 slice. The times are simulated.
32 devices in a mesh: dp: 4 (over x, core), seq: 8 (over z, y).
Axes of the slice: x: 2, y: 2, z: 4, core: 2. Of those that a mesh axis runs over, the one named last changes fastest.
Arguments:
- tokens: bfloat16 [32768, 1152], P(('dp', 'seq')), may hold values from -6 to 6
- condition: bfloat16 [128, 1152], P('dp'), may hold values from -6 to 6
- lengths: int32 [128], P(('dp', 'seq')), may hold values from 1 to 256, 22937 in all
- kept_index: int32 [128, 256], P(('dp', 'seq')), may hold values from 0 to 255, each once within a row
- heads_weight: bfloat16 [1152, 3456], P('seq'), may hold values from -0.1875 to 0.1875
- heads_bias: bfloat16 [2304], replicated, may hold values from -1.5 to 1.5
- merge_weight: bfloat16 [1152, 1152], P('seq'), may hold values from -1.5 to 1.5
- merge_bias: bfloat16 [1152], replicated, may hold values from -4 to 4
- up_weight: bfloat16 [1152, 4608], P('seq'), may hold values from -0.1875 to 0.1875
- up_bias: bfloat16 [4608], replicated, may hold values from -4 to 4
- down_weight: bfloat16 [1152, 4608], P('seq'), may hold values from -0.1875 to 0.1875
- down_bias: bfloat16 [1152], replicated, may hold values from -4 to 4
- modulate_weight: bfloat16 [1152, 6912], P('seq'), may hold values from -0.1875 to 0.1875
- modulate_bias: bfloat16 [6912], replicated, may hold values from -4 to 4
- relative_table: bfloat16 [16, 961], replicated, may hold values from -6 to 6
- cotangent: bfloat16 [32768, 1152], P(('dp', 'seq')), may hold values from -6 to 6
Outputs:
- output: bfloat16 [32768, 1152], P(('dp', 'seq'))
- tokens_grad: float32 [32768, 1152], P(('dp', 'seq'))
- heads_weight_grad: float32 [1152, 3456], P('seq')
- merge_weight_grad: float32 [1152, 1152], P('seq')
- up_weight_grad: float32 [1152, 4608], P('seq')
- down_weight_grad: float32 [1152, 4608], P('seq')
- modulate_weight_grad: float32 [1152, 6912], P('seq')
- heads_bias_grad: float32 [2304], replicated
- merge_bias_grad: float32 [1152], replicated
- up_bias_grad: float32 [4608], replicated
- down_bias_grad: float32 [1152], replicated
- modulate_bias_grad: float32 [6912], replicated
- relative_table_grad: float32 [16, 961], replicated
Inputs may be any that keep to these rules, and one draw needn't show every extreme that they name: The first lengths[s] slots of sample s hold its kept tokens, the rest are empty. Each sample's row is a permutation of the 256 patch positions; slot r's patch lies at row kept_index // 16, column kept_index % 16.
All inputs are finite; a program needn't handle non-finite values. No bound on the sum of `lengths` on one device may be relied on, other than what follows from the above.
Results may differ from a plain program's by a relative error of at most 0.019.
Values may be sent and summed in bfloat16 or wider, within the bound.
No kernel may reach another device: no remote copies, remote signals or barrier semaphores. Data moves between devices by JAX's collectives and lax.ppermute only.
A program may use at most 320 MiB of HBM per device.

v0:
```python
from functools import partial
import math
import jax
import jax.numpy as jnp
from jax import lax
from jax.sharding import PartitionSpec as P

D = 1152
HEADS = 16
HEAD = 72
FF = 4608
SIDE = 16
MICRO = 2
SAMP_DEV = 4
GRID = 256
epsilon = 1e-06


def layer_norm(values):
    center = values - jnp.mean(values, axis=-1, keepdims=True)
    spread = jnp.mean(center * center, axis=-1, keepdims=True)
    return center * lax.rsqrt(spread + epsilon)


def modulated(values, scales, shifts):
    return layer_norm(values) * (1.0 + scales) + shifts


def gelu_tanh(values):
    return jax.nn.gelu(values, approximate=True)


def fold_rows(left, portion):
    return jnp.dot(left, portion, preferred_element_type=jnp.float32)


def right_transposed(left, portion):
    return lax.dot_general(
        left, portion, (((1,), (1,)), ((), ())), preferred_element_type=jnp.float32
    )


def column_outer(left, right):
    return lax.dot_general(
        left, right, (((0,), (0,)), ((), ())), preferred_element_type=jnp.float32
    )


def relative_index(positions):
    row_place = positions // SIDE
    col_place = positions % SIDE
    row_gap = row_place[..., :, None] - row_place[..., None, :] + (SIDE - 1)
    col_gap = col_place[..., :, None] - col_place[..., None, :] + (SIDE - 1)
    return row_gap * (2 * SIDE - 1) + col_gap


def slot_onehot(index_pair):
    return (index_pair[..., :, None] == jnp.arange(GRID)[None, None, :]).astype(jnp.bfloat16)


def pair_scores(packed, lens_pair, index_pair, position_bias):
    parts = packed.reshape(2, GRID, 3, HEADS, HEAD)
    queries = parts[:, :, 0]
    key_part = parts[:, :, 1]
    value_part = parts[:, :, 2]
    scaling = 1.0 / math.sqrt(HEAD)
    onehot = slot_onehot(index_pair)
    rows_placed = jnp.einsum(
        "srp,hpq->hsrq", onehot, position_bias, preferred_element_type=jnp.float32
    ).astype(jnp.bfloat16)
    bias_pair = jnp.einsum(
        "hsrq,skq->hsrk", rows_placed, onehot, preferred_element_type=jnp.float32
    )
    scores = (
        jnp.einsum("sqhe,skhe->hsqk", queries, key_part, preferred_element_type=jnp.float32)
        * scaling
    )
    scores = scores + bias_pair
    living = jnp.arange(GRID)[None, :] < lens_pair[:, None]
    scores = jnp.where(living[None, :, None, :], scores, -1e30)
    return (scores, queries, key_part, value_part, onehot)


def attend_pair(arguments, position_bias):
    packed, lens_pair, index_pair = arguments
    scores, queries, key_part, value_part, onehot = pair_scores(
        packed, lens_pair, index_pair, position_bias
    )
    peak = jnp.max(scores, axis=-1, keepdims=True)
    expo = jnp.exp(scores - peak)
    mass = jnp.sum(expo, axis=-1, keepdims=True)
    probs_low = (expo / mass).astype(jnp.bfloat16)
    mixed = jnp.einsum("hsqk,skhe->sqhe", probs_low, value_part, preferred_element_type=jnp.float32)
    return (mixed.astype(jnp.bfloat16).reshape(2 * GRID, D), (peak + jnp.log(mass))[..., 0])


def attend_pair_back(arguments, position_bias):
    packed, lens_pair, index_pair, logsum, grad_mixed = arguments
    scores, queries, key_part, value_part, onehot = pair_scores(
        packed, lens_pair, index_pair, position_bias
    )
    probs = jnp.exp(scores - logsum[..., None])
    grad_mixed = grad_mixed.reshape(2, GRID, HEADS, HEAD)
    grad_probs = jnp.einsum(
        "sqhe,skhe->hsqk", grad_mixed, value_part, preferred_element_type=jnp.float32
    )
    inner = jnp.sum(probs * grad_probs, axis=-1, keepdims=True)
    grad_scores = (probs * (grad_probs - inner)).astype(jnp.bfloat16)
    scaling = 1.0 / math.sqrt(HEAD)
    grad_query = (
        jnp.einsum("hsqk,skhe->sqhe", grad_scores, key_part, preferred_element_type=jnp.float32)
        * scaling
    )
    grad_key = (
        jnp.einsum("hsqk,sqhe->skhe", grad_scores, queries, preferred_element_type=jnp.float32)
        * scaling
    )
    grad_value = jnp.einsum(
        "hsqk,sqhe->skhe",
        probs.astype(jnp.bfloat16),
        grad_mixed,
        preferred_element_type=jnp.float32,
    )
    stacked = (
        jnp.stack([grad_query, grad_key, grad_value], axis=2)
        .astype(jnp.bfloat16)
        .reshape(2 * GRID, 3 * D)
    )
    rows_back = jnp.einsum(
        "hsrk,srp->hspk", grad_scores, onehot, preferred_element_type=jnp.float32
    ).astype(jnp.bfloat16)
    placed_grad = jnp.einsum("hspk,skq->hpq", rows_back, onehot, preferred_element_type=jnp.float32)
    return (stacked, placed_grad)


def offsets_table(placed_grad):
    spots = jnp.arange(SIDE)
    reach = jnp.arange(2 * SIDE - 1)
    gaps = (
        spots[:, None, None] - spots[None, :, None] + (SIDE - 1) == reach[None, None, :]
    ).astype(jnp.float32)
    grid_grad = placed_grad.reshape(HEADS, SIDE, SIDE, SIDE, SIDE)
    by_rows = jnp.einsum("hwxyz,wya->haxz", grid_grad, gaps, precision=lax.Precision.HIGHEST)
    return jnp.einsum("haxz,xzb->hab", by_rows, gaps, precision=lax.Precision.HIGHEST).reshape(
        HEADS, (2 * SIDE - 1) ** 2
    )


def local(
    tokens,
    condition,
    lengths,
    kept_index,
    heads_weight,
    heads_bias,
    merge_weight,
    merge_bias,
    up_weight,
    up_bias,
    down_weight,
    down_bias,
    modulate_weight,
    modulate_bias,
    relative_table,
    cotangent,
):
    position = lax.axis_index("seq")
    position_bias = jnp.take(relative_table, relative_index(jnp.arange(GRID)), axis=1)
    own_cond = lax.dynamic_slice_in_dim(condition, position * SAMP_DEV, SAMP_DEV, 0)
    own_silu = jax.nn.silu(own_cond.astype(jnp.float32)).astype(jnp.bfloat16)
    modulation = fold_rows(own_silu, lax.all_gather(modulate_weight, "seq", axis=0, tiled=True))
    modulation = (modulation + modulate_bias.astype(jnp.float32)).reshape(SAMP_DEV, 1, 6, D)
    full_bias = jnp.concatenate(
        [heads_bias[:D], jnp.zeros((D,), jnp.bfloat16), heads_bias[D:]]
    ).astype(jnp.float32)
    parts_count = MICRO
    samples = SAMP_DEV // parts_count
    rows = samples * GRID
    pairs = samples // 2
    kept = {
        "out": [],
        "tgrad": [],
        "mgrad": [],
        "hone": [],
        "gpack": [],
        "attn": [],
        "gbranch": [],
        "htwo": [],
        "gup": [],
        "gmlp": [],
        "act": [],
    }
    placed_total = jnp.zeros((HEADS, GRID, GRID), jnp.float32)
    for part in range(parts_count):
        slab = tokens[part * rows : (part + 1) * rows].astype(jnp.float32).reshape(samples, GRID, D)
        mods = modulation[part * samples : (part + 1) * samples]
        shift_one, scale_one, gate_one, shift_two, scale_two, gate_two = [
            mods[:, :, index] for index in range(6)
        ]
        lens_part = lengths[part * samples : (part + 1) * samples]
        index_part = kept_index[part * samples : (part + 1) * samples]
        living = (jnp.arange(GRID)[None, :] < lens_part[:, None])[:, :, None]
        hidden_one = modulated(slab, scale_one, shift_one).astype(jnp.bfloat16).reshape(rows, D)
        packed = (
            fold_rows(hidden_one, lax.all_gather(heads_weight, "seq", axis=0, tiled=True))
            + full_bias
        ).astype(jnp.bfloat16)
        packed_pairs = packed.reshape(pairs, 2 * GRID, 3 * D)
        lens_pairs = lens_part.reshape(pairs, 2)
        index_pairs = index_part.reshape(pairs, 2, GRID)
        attended, logsum = lax.map(
            partial(attend_pair, position_bias=position_bias),
            (packed_pairs, lens_pairs, index_pairs),
        )
        attended = attended.reshape(rows, D)
        branch = fold_rows(
            attended, lax.all_gather(merge_weight, "seq", axis=0, tiled=True)
        ) + merge_bias.astype(jnp.float32)
        branch = branch.reshape(samples, GRID, D)
        middle = slab + gate_one * branch
        hidden_two = modulated(middle, scale_two, shift_two).astype(jnp.bfloat16).reshape(rows, D)
        up_value = fold_rows(
            hidden_two, lax.all_gather(up_weight, "seq", axis=0, tiled=True)
        ) + up_bias.astype(jnp.float32)
        activated = gelu_tanh(up_value).astype(jnp.bfloat16)
        mlp_out = right_transposed(
            activated, lax.all_gather(down_weight, "seq", axis=0, tiled=True)
        )
        mlp_out = (mlp_out + down_bias.astype(jnp.float32)).reshape(samples, GRID, D)
        final = jnp.where(living, middle + gate_two * mlp_out, 0.0)
        kept["out"].append(final.astype(jnp.bfloat16).reshape(rows, D))
        grad_final = jnp.where(
            living,
            cotangent[part * rows : (part + 1) * rows]
            .astype(jnp.float32)
            .reshape(samples, GRID, D),
            0.0,
        )
        gate_two_grad = jnp.sum(grad_final * mlp_out, axis=1, keepdims=True)
        grad_mlp = (gate_two * grad_final).astype(jnp.bfloat16).reshape(rows, D)
        grad_act = fold_rows(grad_mlp, lax.all_gather(down_weight, "seq", axis=0, tiled=True))
        grad_up = jax.vjp(gelu_tanh, up_value)[1](grad_act)[0].astype(jnp.bfloat16)
        grad_hidden_two = right_transposed(
            grad_up, lax.all_gather(up_weight, "seq", axis=0, tiled=True)
        )
        middle_ln, scale_two_grad, shift_two_grad = jax.vjp(
            modulated, middle, scale_two, shift_two
        )[1](grad_hidden_two.reshape(samples, GRID, D))
        grad_middle = grad_final + middle_ln
        gate_one_grad = jnp.sum(grad_middle * branch, axis=1, keepdims=True)
        grad_branch = (gate_one * grad_middle).astype(jnp.bfloat16).reshape(rows, D)
        grad_attended = right_transposed(
            grad_branch, lax.all_gather(merge_weight, "seq", axis=0, tiled=True)
        ).astype(jnp.bfloat16)
        grad_packed, placed_parts = lax.map(
            partial(attend_pair_back, position_bias=position_bias),
            (
                packed_pairs,
                lens_pairs,
                index_pairs,
                logsum,
                grad_attended.reshape(pairs, 2 * GRID, D),
            ),
        )
        grad_packed = grad_packed.reshape(rows, 3 * D)
        placed_total = placed_total + jnp.sum(placed_parts, axis=0)
        grad_hidden_one = right_transposed(
            grad_packed, lax.all_gather(heads_weight, "seq", axis=0, tiled=True)
        )
        slab_ln, scale_one_grad, shift_one_grad = jax.vjp(modulated, slab, scale_one, shift_one)[1](
            grad_hidden_one.reshape(samples, GRID, D)
        )
        kept["tgrad"].append((grad_middle + slab_ln).reshape(rows, D))
        kept["mgrad"].append(
            jnp.concatenate(
                [
                    shift_one_grad,
                    scale_one_grad,
                    gate_one_grad,
                    shift_two_grad,
                    scale_two_grad,
                    gate_two_grad,
                ],
                axis=-1,
            ).reshape(samples, 6 * D)
        )
        kept["hone"].append(hidden_one)
        kept["gpack"].append(grad_packed)
        kept["attn"].append(attended)
        kept["gbranch"].append(grad_branch)
        kept["htwo"].append(hidden_two)
        kept["gup"].append(grad_up)
        kept["gmlp"].append(grad_mlp)
        kept["act"].append(activated)
    table_grad = offsets_table(placed_total)
    joined = {name: jnp.concatenate(items, axis=0) for name, items in kept.items()}
    mod_grad = joined["mgrad"].astype(jnp.bfloat16)
    pieces = [
        column_outer(joined["hone"], joined["gpack"]),
        column_outer(joined["attn"], joined["gbranch"]),
        column_outer(joined["htwo"], joined["gup"]),
        column_outer(joined["gmlp"], joined["act"]),
        column_outer(own_silu, mod_grad),
    ]
    summed = lax.psum_scatter(
        jnp.concatenate(pieces, axis=1).astype(jnp.bfloat16), "seq", scatter_dimension=0, tiled=True
    )
    share = lax.psum_scatter(summed, "dp", scatter_dimension=0, tiled=True).astype(jnp.float32)
    replicated = lax.all_gather(share.astype(jnp.bfloat16), "dp", axis=0, tiled=True).astype(
        share.dtype
    )
    packed_sums = jnp.sum(joined["gpack"], axis=0, dtype=jnp.float32)
    heads_part = jnp.concatenate([packed_sums[:D], packed_sums[2 * D :]])
    merge_part = jnp.sum(joined["gbranch"], axis=0, dtype=jnp.float32)
    up_part = jnp.sum(joined["gup"], axis=0, dtype=jnp.float32)
    down_part = jnp.sum(joined["gmlp"], axis=0, dtype=jnp.float32)
    modulate_part = jnp.sum(mod_grad, axis=0, dtype=jnp.float32)
    heads_total, merge_total, up_total, down_total, modulate_total, table_total = lax.psum(
        (heads_part, merge_part, up_part, down_part, modulate_part, table_grad), ("dp", "seq")
    )
    edges = [0, 3 * D, 4 * D, 4 * D + FF, 4 * D + 2 * FF, 10 * D + 2 * FF]
    return (
        joined["out"],
        joined["tgrad"],
        replicated[:, edges[0] : edges[1]],
        replicated[:, edges[1] : edges[2]],
        replicated[:, edges[2] : edges[3]],
        replicated[:, edges[3] : edges[4]],
        replicated[:, edges[4] : edges[5]],
        heads_total,
        merge_total,
        up_total,
        down_total,
        modulate_total,
        table_total,
    )


def solution(mesh):
    in_specs = (
        P(("dp", "seq"), None),
        P("dp", None),
        P(("dp", "seq")),
        P(("dp", "seq"), None),
        P("seq", None),
        P(),
        P("seq", None),
        P(),
        P("seq", None),
        P(),
        P("seq", None),
        P(),
        P("seq", None),
        P(),
        P(),
        P(("dp", "seq"), None),
    )
    out_specs = (
        P(("dp", "seq"), None),
        P(("dp", "seq"), None),
        P("seq", None),
        P("seq", None),
        P("seq", None),
        P("seq", None),
        P("seq", None),
        P(),
        P(),
        P(),
        P(),
        P(),
        P(),
    )
    return jax.shard_map(local, mesh=mesh, in_specs=in_specs, out_specs=out_specs, check_vma=False)
```

profile of v0, /device:TPU:8, one launch (start us, length us, event | category | flops | bytes accessed | tf_op | source)
XLA Modules:
  0.0 2067.6 jit_solution(3447131822799105786)
XLA Ops:
  26.2 227.7 %gather_fusion = bf16[65536,16]{1,0:T(8,128)(2,1)} fusion(bf16[16,961]{0,1:T(8,128)(2,1)S(1)} %copy.147, s32[65536]{0:T(1024)S(1)} %broadcast_clamp_fusion), kind=kCustom, calls=%fused_computation | custom fusion | bytes 4456448 | tf_op jit(solution)/shard_map/jit(_take)/gather | solution.py:168
  253.8 16.7 copy.148
  292.3 54.5 %all-gather.10.cloned.1.call-done = bf16[1152,3456]{1,0:T(8,128)(2,1)} async-done(((bf16[144,3456]{1,0:T(8,128)(2,1)}), bf16[1152,3456]{1,0:T(8,128)(2,1)}) %all-gather.10.cloned.1.call-update) | async-done | bytes 7962640 | tf_op jit(solution)/shard_map/all_gather | solution.py:205
  370.4 15.9 fusion.217
  411.4 11.2 add_convert_fusion
  467.8 87.5 %all-gather.14.cloned.1.call-done = bf16[1152,4608]{1,0:T(8,128)(2,1)} async-done(((bf16[144,4608]{1,0:T(8,128)(2,1)}), bf16[1152,4608]{1,0:T(8,128)(2,1)}) %all-gather.14.cloned.1.call-update) | async-done | bytes 10616848 | tf_op jit(solution)/shard_map/all_gather | solution.py:223
  555.3 11.7 fusion.231
  575.8 132.2 %all-gather.16.cloned.1.call-done = bf16[1152,4608]{1,0:T(8,128)(2,1)} async-done(((bf16[144,4608]{1,0:T(8,128)(2,1)}), bf16[1152,4608]{1,0:T(8,128)(2,1)}) %all-gather.16.cloned.1.call-update) | async-done | bytes 10616848 | tf_op jit(solution)/shard_map/all_gather | solution.py:227
  708.0 11.6 fusion.232
  719.6 24.2 %fusion.11 = (bf16[512,4608]{1,0:T(8,128)(2,1)}, bf16[512,4608]{1,0:T(8,128)(2,1)}, bf16[512,4608]{1,0:T(8,128)(2,1)}, bf16[512,4608]{1,0:T(8,128)(2,1)}) fusion(f32[512,4608]{1,0:T(8,128)} %fusion.230, f32[4608]{0:T(1024)S(1)} %copy-done.104, f32[512,4608]{1,0:T(8,128)} %fusion.231, f32[512,4608]{1,0:T(8,128)} %fusion.232, ...), kind=kOutput, calls=%fused_computation.21 | convolution fusion | flops 5544345600 | bytes 59000832 | tf_op jit(solution)/shard_map/dot_general | solution.py:34
  743.8 12.7 multiply_reduce_fusion.11
  757.2 13.2 multiply_reduce_fusion.9
  771.0 14.4 fusion.210
  785.5 13.1 fusion.211
  916.6 10.9 fusion.4
  931.0 17.3 fusion.3
  948.4 16.6 fusion.2
  984.2 748.7 %reduce-scatter.4.cloned.1.call-done = bf16[144,20736]{1,0:T(8,128)(2,1)} async-done(((bf16[1152,20736]{1,0:T(8,128)(2,1)}), bf16[144,20736]{1,0:T(8,128)(2,1)}) %reduce-scatter.4.cloned.1.call-update) | async-done | bytes 5971984 | tf_op jit(solution)/shard_map/reduce_scatter | solution.py:305
  1732.9 62.0 %fusion = bf16[40,20736]{1,0:T(8,128)(2,1)} fusion(bf16[144,20736]{1,0:T(8,128)(2,1)} %reduce-scatter.4.cloned.1.call-done), kind=kCustom, calls=%all-reduce-scatter | all-reduce-scatter fusion | flops 3317761 | bytes 7631360
  1800.4 17.0 concatenate.72
  1835.4 19.8 add.547
  1855.2 33.3 %fusion.185 = f32[31,16,16,16,1]{0,3,2,4,1:T(8,128)} fusion(f32[16,16,16,16,16]{4,3,2,1,0:T(8,128)} %add.547, s32[16,16]{1,0:T(8,128)S(1)} %subtract_add_fusion), kind=kOutput, calls=%fused_computation.258 | convolution fusion | flops 390078208 | bytes 4703232 | tf_op jit(solution)/shard_map/hwxyz,wya->haxz/dot_general | solution.py:143
  1916.3 10.3 reshape.899
  1938.7 113.8 %all-reduce.5.cloned.1.call-done = (f32[2304]{0:T(1024)}, f32[1152]{0:T(1024)}, f32[4608]{0:T(1024)}, f32[1152]{0:T(1024)}, f32[6912]{0:T(1024)}, /*index=5*/f32[16,961]{1,0:T(8,128)}) async-done(((f32[2304]{0:T(1024)}, f32[1152]{0:T(1024)}, f32[4608]{0:T(1024)}, f32[1152]{0:T(1024)}, f32[6912]{0:T(1024)}, /*index=5*/f32[16,961]{1,0:T(8,128)}), (f32[2304]{0:T(1024)}, f32[1152]{0:T(1024)}, f32[4608]{0:T(1024)}, ...) | async-done | bytes 126032 | tf_op jit(solution)/shard_map/psum | solution.py:318
  (520 shorter events, 354.4 us)
Async XLA Ops:
  7.2 272.5 %all-gather.8.cloned.1.call-start = ((), (), s32[]{:S(2)}) async-start(), calls=%async_computation.1 | async-start | bytes 17915904 | tf_op jit(solution)/shard_map/all_gather | solution.py:171
  7.9 338.8 %all-gather.10.cloned.1.call-start = ((), (), s32[]{:S(2)}) async-start(), calls=%async_computation.2 | async-start | bytes 8957952 | tf_op jit(solution)/shard_map/all_gather | solution.py:205
  8.7 395.3 %all-gather.12.cloned.1.call-start = ((), (), s32[]{:S(2)}) async-start(), calls=%async_computation.3 | async-start | bytes 2985984 | tf_op jit(solution)/shard_map/all_gather | solution.py:217
  9.4 545.9 %all-gather.14.cloned.1.call-start = ((), (), s32[]{:S(2)}) async-start(), calls=%async_computation.4 | async-start | bytes 11943936 | tf_op jit(solution)/shard_map/all_gather | solution.py:223
  10.0 698.0 %all-gather.16.cloned.1.call-start = ((), (), s32[]{:S(2)}) async-start(), calls=%async_computation.5 | async-start | bytes 11943936 | tf_op jit(solution)/shard_map/all_gather | solution.py:227
  10.6 1722.4 %reduce-scatter.4.cloned.1.call-start = ((), (), s32[]{:S(2)}) async-start(), calls=%async_computation.6 | async-start | bytes 53747712 | tf_op jit(solution)/shard_map/reduce_scatter | solution.py:305
  17.2 253.4 %copy-start.135 = (s32[2,256]{1,0:T(2,128)}, s32[2,256]{1,0:T(2,128)S(1)}, u32[]{:S(2)}) copy-start(s32[2,256]{1,0:T(2,128)S(1)} %get-tuple-element.193) | copy-start | bytes 6148
  17.2 370.5 %copy-start.98 = (s32[2,256]{1,0:T(2,128)}, s32[2,256]{1,0:T(2,128)S(1)}, u32[]{:S(2)}) copy-start(s32[2,256]{1,0:T(2,128)S(1)} %get-tuple-element.192) | copy-start | bytes 6148
  292.3 64.0 %copy-start.63 = (bf16[512,1152]{1,0:T(8,128)(2,1)}, bf16[512,1152]{1,0:T(8,128)(2,1)S(1)}, u32[]{:S(2)}) copy-start(bf16[512,1152]{1,0:T(8,128)(2,1)S(1)} %fusion.98) | copy-start | bytes 3538948
  461.2 309.8 %copy-start.74 = (f32[2,1152]{1,0:T(2,128)}, f32[2,1152]{1,0:T(2,128)S(1)}, u32[]{:S(2)}) copy-start(f32[2,1152]{1,0:T(2,128)S(1)} %get-tuple-element.239) | copy-start | bytes 27652
  464.0 321.5 %copy-start.81 = (f32[2,1152]{1,0:T(2,128)}, f32[2,1152]{1,0:T(2,128)S(1)}, u32[]{:S(2)}) copy-start(f32[2,1152]{1,0:T(2,128)S(1)} %get-tuple-element.235) | copy-start | bytes 27652
  771.0 14.5 copy-start.10
  771.0 14.5 copy-start.11
  771.0 14.5 copy-start.106
  771.0 14.5 copy-start.147
  785.5 14.2 copy-start.71
  931.0 17.3 copy-start.52
  948.3 16.7 copy-start.75
  948.3 16.7 copy-start.126
  948.3 16.7 copy-start.134
  984.2 815.0 %copy-start.154 = (u32[32]{0:T(128)S(1)}, u32[32]{0:T(128)}, u32[]{:S(2)}) copy-start(u32[32]{0:T(128)} %constant.195) | copy-start | bytes 388
  984.2 932.1 %all-gather.18.cloned.1.call-start = ((), (), s32[]{:S(2)}) async-start(), calls=%async_computation.7 | async-start | bytes 8294400 | tf_op jit(solution)/shard_map/all_gather | solution.py:309
  1797.0 3.4 collective-permute-start
  1820.5 232.0 %all-reduce.5.cloned.1.call-start = ((), (), s32[]{:S(2)}) async-start(), calls=%async_computation.8 | async-start | bytes 286720 | tf_op jit(solution)/shard_map/psum | solution.py:318
  (147 other events, 714.2 us)
Sparse Core Ops, SparseCore 0:
  10.2 216.5 all-gather.7
  228.9 117.7 all-gather.9
  348.9 55.0 all-gather.11
  406.0 149.1 all-gather.13
  557.3 150.6 all-gather.15
  984.3 748.6 reduce-scatter.3
  1820.6 57.1 all-gather.17
  1916.3 136.0 all-reduce.4
where the time goes:
time: 2070 us
  waiting for transfers between devices  1140 us (55%)
  local copies, waits for them, and re-layouts  442 us (21%)
  matrix products  327 us (16%)
  other arithmetic  72.9 us (4%)
  blocking collectives  62 us (3%)
    reduce_scatter x1, waiting for transfers between devices, local(): lax.psum_scatter(jnp.concatenate(pieces, axis=1).astype(jnp.bfloat16), 's...  749 us
    gather x2, local copies, waits for them, and re-layouts, local(): jnp.take(relative_table, relative_index(jnp.arange(GRID)), axis=1)  244 us
    all_gather x1, waiting for transfers between devices, local(): lax.all_gather(down_weight, 'seq', axis=0, tiled=True)  132 us
    psum x1, waiting for transfers between devices, local(): lax.psum((heads_part, merge_part, up_part, down_part, modulate_part, tabl...  114 us
    dot_general x9, matrix products, fold_rows(): return jnp.dot(left, portion, preferred_element_type=jnp.float32)  96.1 us
    all_gather x1, waiting for transfers between devices, local(): lax.all_gather(up_weight, 'seq', axis=0, tiled=True)  87.5 us
    dot_general x8, matrix products, right_transposed(): lax.dot_general(left, portion, (((1,), (1,)), ((), ())), preferred_elemen...  77.3 us
    unnamed x359, local copies, waits for them, and re-layouts  65.2 us
  transfers between devices with their start and end apart: 9, of which 6 were waited for; matrix products, arithmetic and copies ran while one was open for 25% of the time, Pallas kernels for 0%

commit v1 on v0

--- a/solution.py
+++ b/solution.py
@@ -14,6 +14,28 @@
 SAMP_DEV = 4
 GRID = 256
 epsilon = 1e-06
+
+
+def laid_out(blocks, dim):
+    blocks = jnp.moveaxis(blocks, 0, dim)
+    shape = blocks.shape
+    return blocks.reshape(*shape[:dim], shape[dim] * shape[dim + 1], *shape[dim + 2 :])
+
+
+def ring_gather(x, axis, dim):
+    devices = lax.axis_size(axis)
+    pairs = [(i, (i + 1) % devices) for i in range(devices)]
+    back = [(b, a) for a, b in pairs]
+    lower, upper = ([], [])
+    for turn in range(devices - 1):
+        if turn % 2 == 0:
+            lower.append(lax.ppermute(lower[-1] if lower else x, axis, pairs))
+        else:
+            upper.append(lax.ppermute(upper[-1] if upper else x, axis, back))
+    blocks = jnp.stack([*lower[::-1], x, *upper])
+    shift = lax.axis_index(axis) - len(lower)
+    blocks = blocks[(jnp.arange(devices) - shift) % devices]
+    return laid_out(blocks, dim)
 
 
 def layer_norm(values):
@@ -201,10 +223,9 @@
         index_part = kept_index[part * samples : (part + 1) * samples]
         living = (jnp.arange(GRID)[None, :] < lens_part[:, None])[:, :, None]
         hidden_one = modulated(slab, scale_one, shift_one).astype(jnp.bfloat16).reshape(rows, D)
-        packed = (
-            fold_rows(hidden_one, lax.all_gather(heads_weight, "seq", axis=0, tiled=True))
-            + full_bias
-        ).astype(jnp.bfloat16)
+        packed = (fold_rows(hidden_one, ring_gather(heads_weight, "seq", 0)) + full_bias).astype(
+            jnp.bfloat16
+        )
         packed_pairs = packed.reshape(pairs, 2 * GRID, 3 * D)
         lens_pairs = lens_part.reshape(pairs, 2)
         index_pairs = index_part.reshape(pairs, 2, GRID)

time: 2070 us -> 2030 us (0.981)
  waiting for transfers between devices: 1140 us -> 1080 us
    ppermute x0 -> x7, waiting for transfers between devices: none -> 116 us  [the longest x4 99.4 us: ring_gather(): lower.append(lax.ppermute(lower[-1] if lower else x, axis, pairs))]
    all_gather x1, waiting for transfers between devices: 87.5 us -> 0.01 us  [local(): lax.all_gather(up_weight, 'seq', axis=0, tiled=True)]
    all_gather x1, waiting for transfers between devices: 54.5 us -> 0.01 us  [local(): lax.all_gather(heads_weight, 'seq', axis=0, tiled=True)]
    all_gather x1, waiting for transfers between devices: 132 us -> 102 us  [local(): lax.all_gather(down_weight, 'seq', axis=0, tiled=True)]
    unnamed x359 -> x367, local copies, waits for them, and re-layouts: 65.2 us -> 75.7 us
  transfers between devices with their start and end apart: 9 -> 16, of which waited for: 6 -> 8; matrix products, arithmetic and copies ran while one was open for 25% -> 35% of each run, Pallas kernels for 0% -> 0%
where the time goes in v1:
time: 2030 us; the launch traced here: 2020 us
  waiting for transfers between devices  1080 us (53%)
  local copies, waits for them, and re-layouts  452 us (22%)
  matrix products  326 us (16%)
  other arithmetic  71.1 us (4%)
  blocking collectives  61.9 us (3%)
    reduce_scatter x1, waiting for transfers between devices, local(): lax.psum_scatter(jnp.concatenate(pieces, axis=1).astype(jnp.bfloat16), 's...  749 us
    gather x2, local copies, waits for them, and re-layouts, local(): jnp.take(relative_table, relative_index(jnp.arange(GRID)), axis=1)  244 us
    psum x1, waiting for transfers between devices, local(): lax.psum((heads_part, merge_part, up_part, down_part, modulate_part, tabl...  114 us
    all_gather x1, waiting for transfers between devices, local(): lax.all_gather(down_weight, 'seq', axis=0, tiled=True)  102 us
    ppermute x4, waiting for transfers between devices, ring_gather(): lower.append(lax.ppermute(lower[-1] if lower else x, axis, pairs))  99.4 us
    dot_general x9, matrix products, fold_rows(): return jnp.dot(left, portion, preferred_element_type=jnp.float32)  95.2 us
    dot_general x8, matrix products, right_transposed(): lax.dot_general(left, portion, (((1,), (1,)), ((), ())), preferred_elemen...  80.6 us
    unnamed x367, local copies, waits for them, and re-layouts  75.7 us
  transfers between devices with their start and end apart: 16, of which 8 were waited for; matrix products, arithmetic and copies ran while one was open for 35% of the time, Pallas kernels for 0%

profile of v1, /device:TPU:8, one launch (start us, length us, event | category | flops | bytes accessed | tf_op | source)
XLA Modules:
  0.0 2024.1 jit_solution(4371605128149297503)
XLA Ops:
  21.0 227.3 %gather_fusion.1 = bf16[65536,16]{1,0:T(8,128)(2,1)} fusion(bf16[16,961]{0,1:T(8,128)(2,1)S(1)} %copy.147, s32[65536]{0:T(1024)S(1)} %broadcast_clamp_fusion), kind=kCustom, calls=%fused_computation.1 | custom fusion | bytes 4456448 | tf_op jit(solution)/shard_map/jit(_take)/gather | solution.py:190
  248.3 16.8 copy.148
  266.1 38.7 %collective-permute-done.1 = bf16[144,3456]{1,0:T(8,128)(2,1)S(1)} collective-permute-done((bf16[144,3456]{1,0:T(8,128)(2,1)}, bf16[144,3456]{1,0:T(8,128)(2,1)S(1)}, u32[]{:S(2)}, u32[]{:S(2)}) %collective-permute-start.1) | collective-permute-done | bytes 995360 | tf_op jit(solution)/shard_map/ppermute | solution.py:32
  315.0 44.6 %collective-permute-done.2 = bf16[144,3456]{1,0:T(8,128)(2,1)S(1)} collective-permute-done((bf16[144,3456]{1,0:T(8,128)(2,1)S(1)}, bf16[144,3456]{1,0:T(8,128)(2,1)S(1)}, u32[]{:S(2)}, u32[]{:S(2)}) %collective-permute-start.2) | collective-permute-done | bytes 995360 | tf_op jit(solution)/shard_map/ppermute | solution.py:32
  367.9 14.6 collective-permute-done.5
  382.6 16.1 collective-permute-done.3
  538.9 11.9 fusion.233
  559.6 102.3 %all-gather.14.cloned.1.call-done = bf16[1152,4608]{1,0:T(8,128)(2,1)} async-done(((bf16[144,4608]{1,0:T(8,128)(2,1)}), bf16[1152,4608]{1,0:T(8,128)(2,1)}) %all-gather.14.cloned.1.call-update) | async-done | bytes 10616848 | tf_op jit(solution)/shard_map/all_gather | solution.py:248
  661.8 11.7 fusion.234
  673.5 24.4 %fusion.11 = (bf16[512,4608]{1,0:T(8,128)(2,1)}, bf16[512,4608]{1,0:T(8,128)(2,1)}, bf16[512,4608]{1,0:T(8,128)(2,1)}, bf16[512,4608]{1,0:T(8,128)(2,1)}) fusion(f32[512,4608]{1,0:T(8,128)} %fusion.232, f32[4608]{0:T(1024)S(1)} %copy-done.98, f32[512,4608]{1,0:T(8,128)} %fusion.233, f32[512,4608]{1,0:T(8,128)} %fusion.234, ...), kind=kOutput, calls=%fused_computation.22 | convolution fusion | flops 5544345600 | bytes 59000832 | tf_op jit(solution)/shard_map/dot_general | solution.py:56
  697.9 12.9 multiply_reduce_fusion.11
  711.5 13.7 multiply_reduce_fusion.9
  725.8 14.4 fusion.213
  740.9 14.3 fusion.212
  872.6 10.9 fusion.4
  887.0 17.2 fusion.3
  904.2 16.6 fusion.2
  939.9 749.3 %reduce-scatter.4.cloned.1.call-done = bf16[144,20736]{1,0:T(8,128)(2,1)} async-done(((bf16[1152,20736]{1,0:T(8,128)(2,1)}), bf16[144,20736]{1,0:T(8,128)(2,1)}) %reduce-scatter.4.cloned.1.call-update) | async-done | bytes 5971984 | tf_op jit(solution)/shard_map/reduce_scatter | solution.py:326
  1689.2 61.9 %fusion = bf16[40,20736]{1,0:T(8,128)(2,1)} fusion(bf16[144,20736]{1,0:T(8,128)(2,1)} %reduce-scatter.4.cloned.1.call-done), kind=kCustom, calls=%all-reduce-scatter | all-reduce-scatter fusion | flops 3317761 | bytes 7631360
  1756.6 17.0 concatenate.72
  1791.7 20.2 add.576
  1811.9 33.3 %fusion.185 = f32[31,16,16,16,1]{0,3,2,4,1:T(8,128)} fusion(f32[16,16,16,16,16]{4,3,2,1,0:T(8,128)} %add.576, s32[16,16]{1,0:T(8,128)S(1)} %subtract_add_fusion), kind=kOutput, calls=%fused_computation.267 | convolution fusion | flops 390078208 | bytes 4703232 | tf_op jit(solution)/shard_map/hwxyz,wya->haxz/dot_general | solution.py:165
  1872.8 10.3 reshape.961
  1895.2 113.8 %all-reduce.5.cloned.1.call-done = (f32[2304]{0:T(1024)}, f32[1152]{0:T(1024)}, f32[4608]{0:T(1024)}, f32[1152]{0:T(1024)}, f32[6912]{0:T(1024)}, /*index=5*/f32[16,961]{1,0:T(8,128)}) async-done(((f32[2304]{0:T(1024)}, f32[1152]{0:T(1024)}, f32[4608]{0:T(1024)}, f32[1152]{0:T(1024)}, f32[6912]{0:T(1024)}, /*index=5*/f32[16,961]{1,0:T(8,128)}), (f32[2304]{0:T(1024)}, f32[1152]{0:T(1024)}, f32[4608]{0:T(1024)}, ...) | async-done | bytes 126032 | tf_op jit(solution)/shard_map/psum | solution.py:339
  (547 shorter events, 393.0 us)
Async XLA Ops:
  7.2 413.5 %all-gather.8.cloned.1.call-start = ((), (), s32[]{:S(2)}) async-start(), calls=%async_computation.1 | async-start | bytes 17915904 | tf_op jit(solution)/shard_map/all_gather | solution.py:193
  7.9 466.4 %all-gather.10.cloned.1.call-start = ((), (), s32[]{:S(2)}) async-start(), calls=%async_computation.2 | async-start | bytes 2985984 | tf_op jit(solution)/shard_map/all_gather | solution.py:238
  8.7 530.3 %all-gather.12.cloned.1.call-start = ((), (), s32[]{:S(2)}) async-start(), calls=%async_computation.3 | async-start | bytes 11943936 | tf_op jit(solution)/shard_map/all_gather | solution.py:244
  9.4 652.4 %all-gather.14.cloned.1.call-start = ((), (), s32[]{:S(2)}) async-start(), calls=%async_computation.4 | async-start | bytes 11943936 | tf_op jit(solution)/shard_map/all_gather | solution.py:248
  10.0 827.6 %all-gather.16.cloned.1.call-start = ((), (), s32[]{:S(2)}) async-start(), calls=%async_computation.5 | async-start | bytes 8957952 | tf_op jit(solution)/shard_map/all_gather | solution.py:289
  10.0 255.1 %collective-permute-start = (bf16[144,3456]{1,0:T(8,128)(2,1)}, bf16[144,3456]{1,0:T(8,128)(2,1)}, u32[]{:S(2)}, u32[]{:S(2)}) collective-permute-start(bf16[144,3456]{1,0:T(8,128)(2,1)} %param.20), channel_id=1, source_target_pairs={{0,1},{1,2},{2,3},{3,4},{4,5},{5,6},{6,7},{7,0},{8,9},{9,10},{10,1... | collective-permute-start | bytes 2985992 | tf_op jit(solution)/shard_map/ppermute | solution.py:32
  11.6 300.5 %collective-permute-start.4 = (bf16[144,3456]{1,0:T(8,128)(2,1)}, bf16[144,3456]{1,0:T(8,128)(2,1)}, u32[]{:S(2)}, u32[]{:S(2)}) collective-permute-start(bf16[144,3456]{1,0:T(8,128)(2,1)} %param.20), channel_id=1, source_target_pairs={{1,0},{2,1},{3,2},{4,3},{5,4},{6,5},{7,6},{0,7},{9,8},{10,9},{11,1... | collective-permute-start | bytes 2985992 | tf_op jit(solution)/shard_map/ppermute | solution.py:34
  13.0 1676.2 %reduce-scatter.4.cloned.1.call-start = ((), (), s32[]{:S(2)}) async-start(), calls=%async_computation.6 | async-start | bytes 53747712 | tf_op jit(solution)/shard_map/reduce_scatter | solution.py:326
  15.7 446.6 %copy-start.122 = (pred[2,256]{1,0:T(4,128)(4,1)}, pred[2,256]{1,0:T(4,128)(4,1)S(1)}, u32[]{:S(2)}) copy-start(pred[2,256]{1,0:T(4,128)(4,1)S(1)} %get-tuple-element.241) | copy-start | bytes 1540
  265.2 39.6 %collective-permute-start.1 = (bf16[144,3456]{1,0:T(8,128)(2,1)}, bf16[144,3456]{1,0:T(8,128)(2,1)S(1)}, u32[]{:S(2)}, u32[]{:S(2)}) collective-permute-start(bf16[144,3456]{1,0:T(8,128)(2,1)} %collective-permute-done), channel_id=1, source_target_pairs={{0,1},{1,2},{2,3},{3,4},{4,5},{5,6},{6,7},{7,0},{8,9},{9,10},{10,1... | collective-permute-start | bytes 2985992 | tf_op jit(solution)/shard_map/ppermute | solution.py:32
  265.8 166.5 %copy-start.124 = (f32[3456]{0:T(1024)}, f32[3456]{0:T(1024)S(1)}, u32[]{:S(2)}) copy-start(f32[3456]{0:T(1024)S(1)} %maximum_convert_fusion.2) | copy-start | bytes 41476
  265.8 43.9 %copy-start.134 = (s32[2,256]{1,0:T(2,128)}, s32[2,256]{1,0:T(2,128)S(1)}, u32[]{:S(2)}) copy-start(s32[2,256]{1,0:T(2,128)S(1)} %get-tuple-element.193) | copy-start | bytes 6148
  265.8 196.4 %copy-start.95 = (s32[2,256]{1,0:T(2,128)}, s32[2,256]{1,0:T(2,128)S(1)}, u32[]{:S(2)}) copy-start(s32[2,256]{1,0:T(2,128)S(1)} %get-tuple-element.192) | copy-start | bytes 6148
  304.8 54.8 %collective-permute-start.2 = (bf16[144,3456]{1,0:T(8,128)(2,1)S(1)}, bf16[144,3456]{1,0:T(8,128)(2,1)S(1)}, u32[]{:S(2)}, u32[]{:S(2)}) collective-permute-start(bf16[144,3456]{1,0:T(8,128)(2,1)S(1)} %collective-permute-done.1), channel_id=1, source_target_pairs={{0,1},{1,2},{2,3},{3,4},{4,5},{5,6},{6,7},{7,0},{8,9},{9,10},{10,1... | collective-permute-start | bytes 2985992 | tf_op jit(solution)/shard_map/ppermute | solution.py:32
  309.7 52.4 %copy-start.58 = (bf16[256,256,16]{0,1,2:T(8,128)(2,1)S(1)}, bf16[256,256,16]{0,1,2:T(8,128)(2,1)}, u32[]{:S(2)}) copy-start(bf16[256,256,16]{0,1,2:T(8,128)(2,1)} %copy.148) | copy-start | bytes 6291460
  312.1 70.3 %collective-permute-start.5 = (bf16[144,3456]{1,0:T(8,128)(2,1)}, bf16[144,3456]{1,0:T(8,128)(2,1)S(1)}, u32[]{:S(2)}, u32[]{:S(2)}) collective-permute-start(bf16[144,3456]{1,0:T(8,128)(2,1)} %collective-permute-done.4), channel_id=1, source_target_pairs={{1,0},{2,1},{3,2},{4,3},{5,4},{6,5},{7,6},{0,7},{9,8},{10,9},{11,1... | collective-permute-start | bytes 2985992 | tf_op jit(solution)/shard_map/ppermute | solution.py:34
  359.6 39.2 %collective-permute-start.3 = (bf16[144,3456]{1,0:T(8,128)(2,1)S(1)}, bf16[144,3456]{1,0:T(8,128)(2,1)S(1)}, u32[]{:S(2)}, u32[]{:S(2)}) collective-permute-start(bf16[144,3456]{1,0:T(8,128)(2,1)S(1)} %collective-permute-done.2), channel_id=1, source_target_pairs={{0,1},{1,2},{2,3},{3,4},{4,5},{5,6},{6,7},{7,0},{8,9},{9,10},{10,1... | collective-permute-start | bytes 2985992 | tf_op jit(solution)/shard_map/ppermute | solution.py:32
  382.5 29.0 %collective-permute-start.6 = (bf16[144,3456]{1,0:T(8,128)(2,1)S(1)}, bf16[144,3456]{1,0:T(8,128)(2,1)S(1)}, u32[]{:S(2)}, u32[]{:S(2)}) collective-permute-start(bf16[144,3456]{1,0:T(8,128)(2,1)S(1)} %collective-permute-done.5), channel_id=1, source_target_pairs={{1,0},{2,1},{3,2},{4,3},{5,4},{6,5},{7,6},{0,7},{9,8},{10,9},{11,1... | collective-permute-start | bytes 2985992 | tf_op jit(solution)/shard_map/ppermute | solution.py:34
  533.3 207.5 %copy-start.71 = (f32[2,1152]{1,0:T(2,128)}, f32[2,1152]{1,0:T(2,128)S(1)}, u32[]{:S(2)}) copy-start(f32[2,1152]{1,0:T(2,128)S(1)} %get-tuple-element.239) | copy-start | bytes 27652
  533.4 192.4 %copy-start.78 = (f32[2,1152]{1,0:T(2,128)}, f32[2,1152]{1,0:T(2,128)S(1)}, u32[]{:S(2)}) copy-start(f32[2,1152]{1,0:T(2,128)S(1)} %get-tuple-element.235) | copy-start | bytes 27652
  939.9 815.5 %copy-start.154 = (u32[32]{0:T(128)S(1)}, u32[32]{0:T(128)}, u32[]{:S(2)}) copy-start(u32[32]{0:T(128)} %constant.216) | copy-start | bytes 388
  939.9 932.9 %all-gather.18.cloned.1.call-start = ((), (), s32[]{:S(2)}) async-start(), calls=%async_computation.7 | async-start | bytes 8294400 | tf_op jit(solution)/shard_map/all_gather | solution.py:330
  1753.2 3.4 collective-permute-start.7
  1776.8 232.3 %all-reduce.5.cloned.1.call-start = ((), (), s32[]{:S(2)}) async-start(), calls=%async_computation.8 | async-start | bytes 286720 | tf_op jit(solution)/shard_map/psum | solution.py:339
  (154 other events, 940.2 us)
Sparse Core Ops, SparseCore 0:
  10.2 234.5 all-gather.7
  247.0 70.3 all-gather.9
  319.6 189.5 all-gather.11
  511.2 150.6 all-gather.13
  663.9 117.7 all-gather.15
  940.0 749.1 reduce-scatter.3
  1776.9 57.1 all-gather.17
  1872.9 136.0 all-reduce.4
